TPU v7x, 256 devices: a whole 4x4x8 slice. The times are simulated.
256 devices in a mesh: fsdp: 32 (over y, x, core), tp: 8 (over z).
Axes of the slice: x: 4, y: 4, z: 8, core: 2. Of those that a mesh axis runs over, the one named last changes fastest.
Arguments:
- dec_queries: bfloat16 [2, 64, 8192], P(None, 'fsdp', 'tp'), may hold values from -160 to 160
- cache_keys: bfloat16 [64, 4096, 1024], P('fsdp', None, 'tp'), may hold values from -5.2 to 5.2
- cached_value_rows: bfloat16 [64, 4096, 1024], P('fsdp', None, 'tp'), may hold values from -6 to 6
- step_keys: bfloat16 [2, 64, 1024], P(None, 'fsdp', 'tp'), may hold values from -6 to 6
- step_values: bfloat16 [2, 64, 1024], P(None, 'fsdp', 'tp'), may hold values from -6 to 6
- prompt_lengths: int32 [64], P('fsdp'), may hold values from 2 to 4096
- resp_embed: bfloat16 [512, 32, 8192], P('fsdp', None, 'tp'), may hold values from -520 to 520
- resp_ids: int32 [512, 32], P('fsdp'), may hold values from 0 to 152063
- resp_lengths: int32 [512], P('fsdp'), may hold values from 25 to 32
- dest_shard: int32 [512], P('fsdp'), may hold values from 0 to 31, as said below
- dest_offset: int32 [512], P('fsdp'), may hold values from 0 to 511, as said below
- norm_gain: float32 [8192], replicated, may hold values from 0.7 to 7
- w_q: bfloat16 [8192, 8192], P('fsdp', 'tp'), may hold values from -0.0625 to 0.0625
- key_value_weight: bfloat16 [8192, 2, 1024], P('fsdp', None, 'tp'), may hold values from -0.0625 to 0.0625
- bias_q: float32 [8192], P('tp'), may hold values from -3 to 3
- key_value_bias: float32 [2, 1024], P(None, 'tp'), may hold values from -3 to 3
Outputs:
- decode_out: bfloat16 [2, 64, 8192], P(None, 'fsdp', 'tp')
- packed_ids: int32 [16384], P('fsdp')
- ref_attn: bfloat16 [16384, 8192], P('fsdp', 'tp')
Inputs may be any that keep to these rules, and one draw needn't show every extreme that they name: `dest_shard`: each shard receives exactly 16 responses; the 16 responses held by one index of fsdp go 1 each to half of the shards and none to the others. The responses of one shard occupy disjoint runs from dest_offset to dest_offset + resp_lengths - 1 within its 512 positions.
All inputs are finite; a program needn't handle non-finite values.
Results may differ from a plain program's by a relative error of at most 0.005.
The roundings to bfloat16 on the way count: a program that leaves them out, or rounds other values in their place, can miss the bound.
Values may be sent and summed in bfloat16 or wider, within the bound.
No kernel may reach another device: no remote copies, remote signals or barrier semaphores. Data moves between devices by JAX's collectives and lax.ppermute only.
A program may use at most 128 MiB of HBM per device.

v0:
```python
import jax
import jax.numpy as jnp
from jax import lax
from jax.sharding import PartitionSpec as P

QUERY_HEADS = 64
KEY_VALUE_HEADS = 8
HEAD_SIZE = 128
rope_base = 1000000.0
eps_norm = 1e-06


def sent_together(arrays, axis, dim, along):
    ends, at = ([], 0)
    for a in arrays[:-1]:
        at += a.shape[along]
        ends.append(at)
    both = jnp.concatenate(arrays, axis=along)
    return tuple(jnp.split(lax.all_gather(both, axis, axis=dim, tiled=True), ends, axis=along))


def rotate_half(values, positions):
    half_dim = HEAD_SIZE // 2
    frequency = rope_base ** (-jnp.arange(half_dim, dtype=jnp.float32) * 2.0 / HEAD_SIZE)
    angles = positions.astype(jnp.float32)[:, None] * frequency[None, :]
    cosine = jnp.cos(angles)[:, None, :]
    sine_part = jnp.sin(angles)[:, None, :]
    lower_half = values[..., :half_dim]
    upper_half = values[..., half_dim:]
    return jnp.concatenate(
        [
            lower_half * cosine - upper_half * sine_part,
            upper_half * cosine + lower_half * sine_part,
        ],
        axis=-1,
    )


def decode_local(
    dec_queries, cache_keys, cached_value_rows, step_keys, step_values, prompt_lengths
):
    step_count, row_count, head_width = dec_queries.shape
    head_groups = QUERY_HEADS // KEY_VALUE_HEADS
    kv_local = cache_keys.shape[2] // HEAD_SIZE
    length = cache_keys.shape[1]
    score_scale = HEAD_SIZE ** (-0.5)
    query_rows = dec_queries.reshape(step_count, row_count, kv_local, head_groups, HEAD_SIZE)
    key_matrix = cache_keys.reshape(row_count, length, kv_local, HEAD_SIZE)
    value_matrix = cached_value_rows.reshape(row_count, length, kv_local, HEAD_SIZE)
    latest_key = step_keys.reshape(step_count, row_count, kv_local, HEAD_SIZE)
    latest_value = step_values.reshape(step_count, row_count, kv_local, HEAD_SIZE)
    cached = (
        jnp.einsum("srkgd,rckd->srkgc", query_rows, key_matrix, preferred_element_type=jnp.float32)
        * score_scale
    )
    live_mask = jnp.arange(length, dtype=jnp.int32)[None, :] < prompt_lengths[:, None]
    cached = jnp.where(live_mask[None, :, None, None, :], cached, -jnp.inf)
    recent = (
        jnp.einsum("srkgd,urkd->srkgu", query_rows, latest_key, preferred_element_type=jnp.float32)
        * score_scale
    )
    causal = jnp.arange(step_count)[None, :] <= jnp.arange(step_count)[:, None]
    recent = jnp.where(causal[:, None, None, None, :], recent, -jnp.inf)
    highest = jnp.maximum(jnp.max(cached, axis=-1), jnp.max(recent, axis=-1))[..., None]
    cached_w = jnp.exp(cached - highest)
    recent_w = jnp.exp(recent - highest)
    totals = jnp.sum(cached_w, axis=-1, keepdims=True) + jnp.sum(recent_w, axis=-1, keepdims=True)
    cached_w = (cached_w / totals).astype(jnp.bfloat16)
    recent_w = (recent_w / totals).astype(jnp.bfloat16)
    output = jnp.einsum(
        "srkgc,rckd->srkgd", cached_w, value_matrix, preferred_element_type=jnp.float32
    )
    output = output + jnp.einsum(
        "srkgu,urkd->srkgd", recent_w, latest_value, preferred_element_type=jnp.float32
    )
    return output.reshape(step_count, row_count, head_width).astype(jnp.bfloat16)


def attend_packed(query_raw, unscaled_pairs, doc_ids, token_row, covered):
    token_count = query_raw.shape[0]
    kv_count = unscaled_pairs.shape[2] // HEAD_SIZE
    head_groups = QUERY_HEADS // KEY_VALUE_HEADS
    query_rows = rotate_half(
        query_raw.reshape(token_count, kv_count * head_groups, HEAD_SIZE), token_row
    ).astype(jnp.bfloat16)
    key_matrix = rotate_half(
        unscaled_pairs[:, 0].reshape(token_count, kv_count, HEAD_SIZE), token_row
    ).astype(jnp.bfloat16)
    value_matrix = (
        unscaled_pairs[:, 1].reshape(token_count, kv_count, HEAD_SIZE).astype(jnp.bfloat16)
    )
    query_rows = query_rows.reshape(token_count, kv_count, head_groups, HEAD_SIZE)
    scores = jnp.einsum(
        "tkgd,skd->kgts", query_rows, key_matrix, preferred_element_type=jnp.float32
    ) * HEAD_SIZE ** (-0.5)
    indices = jnp.arange(token_count, dtype=jnp.int32)
    allowed = (doc_ids[:, None] == doc_ids[None, :]) & (indices[None, :] <= indices[:, None])
    scores = jnp.where(allowed, scores, -jnp.inf)
    highest = jnp.max(scores, axis=-1, keepdims=True)
    weights = jnp.exp(scores - highest)
    weights = (weights / jnp.sum(weights, axis=-1, keepdims=True)).astype(jnp.bfloat16)
    output = jnp.einsum("kgts,skd->tkgd", weights, value_matrix, preferred_element_type=jnp.float32)
    output = jnp.where(covered[:, None, None, None], output, 0.0)
    return output.reshape(token_count, kv_count * head_groups * HEAD_SIZE).astype(jnp.bfloat16)


def normalize(rows, norm_gain):
    wide = rows.astype(jnp.float32)
    return (
        wide
        * lax.rsqrt(jnp.mean(wide * wide, axis=1, keepdims=True) + eps_norm)
        * norm_gain[None, :]
    ).astype(jnp.bfloat16)


def on_device(
    dec_queries,
    cache_keys,
    cached_value_rows,
    step_keys,
    step_values,
    prompt_lengths,
    resp_embed,
    resp_ids,
    resp_lengths,
    dest_shard,
    dest_offset,
    norm_gain,
    w_q,
    key_value_weight,
    bias_q,
    key_value_bias,
):
    decode_out = decode_local(
        dec_queries, cache_keys, cached_value_rows, step_keys, step_values, prompt_lengths
    )
    nshard = lax.axis_size("fsdp")
    resp_count = resp_lengths.shape[0]
    resp_span = resp_embed.shape[1]
    packed_len = resp_count * resp_span
    capacity = 2 * resp_count // nshard
    indices = jnp.arange(resp_count, dtype=jnp.int32)
    earlier = (dest_shard[None, :] == dest_shard[:, None]) & (indices[None, :] < indices[:, None])
    pair_rank = jnp.sum(earlier.astype(jnp.int32), axis=1)
    placing = (dest_shard[:, None, None] == jnp.arange(nshard, dtype=jnp.int32)[None, :, None]) & (
        pair_rank[:, None, None] == jnp.arange(capacity, dtype=jnp.int32)[None, None, :]
    )
    slot_rows = jnp.einsum(
        "kpc,krx->pcrx",
        placing.astype(jnp.bfloat16),
        resp_embed,
        preferred_element_type=jnp.float32,
    ).astype(jnp.bfloat16)
    slot_ids = jnp.sum(jnp.where(placing[:, :, :, None], resp_ids[:, None, None, :], 0), axis=0)
    slot_lengths = jnp.sum(jnp.where(placing, resp_lengths[:, None, None], 0), axis=0)
    slot_offsets = jnp.sum(jnp.where(placing, dest_offset[:, None, None], 0), axis=0)
    slot_meta = jnp.stack([slot_lengths, slot_offsets], axis=-1)
    arrived, arrived_ids, arrived_meta = (
        lax.all_to_all(slot_rows, "fsdp", split_axis=0, concat_axis=0, tiled=True),
        lax.all_to_all(slot_ids, "fsdp", split_axis=0, concat_axis=0, tiled=True),
        lax.all_to_all(slot_meta, "fsdp", split_axis=0, concat_axis=0, tiled=True),
    )
    slot_total = nshard * capacity
    flat_rows = arrived.reshape(slot_total * resp_span, arrived.shape[3])
    flat_ids = arrived_ids.reshape(slot_total * resp_span)
    lengths_in = arrived_meta[:, :, 0].reshape(slot_total)
    offsets_in = arrived_meta[:, :, 1].reshape(slot_total)
    position = jnp.arange(packed_len, dtype=jnp.int32)
    inside = (position[:, None] >= offsets_in[None, :]) & (
        position[:, None] < (offsets_in + lengths_in)[None, :]
    )
    covered = jnp.any(inside, axis=1)
    slot_pick = jnp.sum(
        jnp.where(inside, jnp.arange(slot_total, dtype=jnp.int32)[None, :], 0), axis=1
    )
    token_row = jnp.where(
        covered, position - jnp.sum(jnp.where(inside, offsets_in[None, :], 0), axis=1), 0
    )
    source_row = jnp.where(covered, slot_pick * resp_span + token_row, 0)
    tokens = jnp.where(covered[:, None], flat_rows[source_row], jnp.zeros((), jnp.bfloat16))
    packed_ids = jnp.where(covered, flat_ids[source_row], -1).astype(jnp.int32)
    doc_ids = jnp.where(covered, slot_pick, -1)
    full_rows = lax.all_gather(tokens, "tp", axis=1, tiled=True)
    scaled_input = normalize(full_rows, norm_gain)
    q_width = w_q.shape[1]
    pair_width = key_value_weight.shape[1] * key_value_weight.shape[2]
    w_pairs = key_value_weight.reshape(key_value_weight.shape[0], pair_width)

    def add_rows(totals, piece_rows, start_row):
        columns = lax.dynamic_slice_in_dim(scaled_input, start_row, piece_rows.shape[0], 1)
        return totals + jnp.dot(columns, piece_rows, preferred_element_type=jnp.float32)

    empty_q = jnp.zeros((packed_len, q_width), jnp.float32)
    empty_pairs = jnp.zeros((packed_len, pair_width), jnp.float32)
    totals = (empty_q, empty_pairs)
    piece_rows = sent_together((w_q, w_pairs), "fsdp", 0, 1)
    start_row = jnp.int32(0)
    query_raw = add_rows(totals[0], piece_rows[0], start_row)
    unscaled_pairs = add_rows(totals[1], piece_rows[1], start_row)
    query_raw = query_raw + bias_q[None, :]
    unscaled_pairs = unscaled_pairs.reshape(packed_len, 2, pair_width // 2) + key_value_bias[None]
    ref_attn = attend_packed(query_raw, unscaled_pairs, doc_ids, token_row, covered)
    return (decode_out, packed_ids, ref_attn)


def solution(mesh):
    in_specs = (
        P(None, "fsdp", "tp"),
        P("fsdp", None, "tp"),
        P("fsdp", None, "tp"),
        P(None, "fsdp", "tp"),
        P(None, "fsdp", "tp"),
        P("fsdp"),
        P("fsdp", None, "tp"),
        P("fsdp", None),
        P("fsdp"),
        P("fsdp"),
        P("fsdp"),
        P(),
        P("fsdp", "tp"),
        P("fsdp", None, "tp"),
        P("tp"),
        P(None, "tp"),
    )
    out_specs = (P(None, "fsdp", "tp"), P("fsdp"), P("fsdp", "tp"))
    return jax.shard_map(
        on_device, mesh=mesh, in_specs=in_specs, out_specs=out_specs, check_vma=False
    )
```

profile of v0, /device:TPU:1, one launch (start us, length us, event | category | flops | bytes accessed | tf_op | source)
XLA Modules:
  0.0 290.8 jit_solution(11311541848920163075)
XLA Ops:
  7.2 0.0 copy-start
  7.2 1.0 convert_reduce_fusion
  8.2 0.8 select_reduce_fusion.4
  9.0 0.7 copy.91
  9.7 8.6 %all-to-all-start = ((s32[32,1,2]{2,1,0:T(1,128)}), s32[32,1,2]{2,1,0:T(1,128)S(1)}, u32[]{:S(2)}, u32[]{:S(2)}) async-start(s32[32,1,2]{2,1,0:T(1,128)} %copy.91), calls=%async_computation | async-start | bytes 32768 | tf_op jit(solution)/shard_map/all_to_all | solution.py:161
  18.3 2.2 convert_bitcast_fusion
  20.5 2.4 copy.94
  22.9 2.2 all-to-all-done
  25.2 5.3 %all-to-all-start.2 = ((bf16[32,1,32,1024]{3,2,1,0:T(8,128)(2,1)}), bf16[32,1,32,1024]{3,2,1,0:T(8,128)(2,1)}, u32[]{:S(2)}, u32[]{:S(2)}) async-start(bf16[32,1,32,1024]{3,2,1,0:T(8,128)(2,1)} %copy.94), calls=%async_computation.2 | async-start | bytes 4194304 | tf_op jit(solution)/shard_map/all_to_all | solution.py:159
  30.5 0.0 copy-start.5
  30.5 0.0 copy-start.3
  30.5 0.0 copy-start.4
  30.5 0.0 copy-start.11
  30.5 0.0 copy-start.8
  30.6 0.0 all-gather.3.cloned.1.call-start
  30.6 1.3 slice_reduce_fusion
  31.9 0.1 fusion.60
  32.0 0.1 select_reduce_fusion.1
  32.1 27.1 %all-to-all-done.2 = bf16[32,1,32,1024]{3,2,1,0:T(8,128)(2,1)} async-done(((bf16[32,1,32,1024]{3,2,1,0:T(8,128)(2,1)}), bf16[32,1,32,1024]{3,2,1,0:T(8,128)(2,1)}, u32[]{:S(2)}, u32[]{:S(2)}) %all-to-all-start.2) | async-done | bytes 2097184 | tf_op jit(solution)/shard_map/all_to_all | solution.py:159
  59.2 4.6 %gather_fusion.1 = bf16[512,1024]{1,0:T(8,128)(2,1)S(1)} fusion(bf16[1024,1024]{1,0:T(8,128)(2,1)} %bitcast.24, s32[1024]{0:T(1024)S(1)} %pad_clamp_fusion), kind=kCustom, calls=%fused_computation.1 | custom fusion | bytes 2099200 | tf_op jit(solution)/shard_map/gather | solution.py:180
  63.8 1.1 broadcast_select_fusion
  65.0 0.0 all-gather.3.cloned.1.call-update
  65.0 0.0 all-gather.5.cloned.1.call-start
  65.1 2.0 pad_maximum_fusion
  67.0 0.0 all-gather.5.cloned.1.call-update
  67.1 0.1 fusion.63
  67.1 0.7 select_reduce_fusion
  67.9 5.1 %all-to-all-start.1 = ((s32[32,1,32]{2,1,0:T(1,128)}), s32[32,1,32]{2,1,0:T(1,128)S(1)}, u32[]{:S(2)}, u32[]{:S(2)}) async-start(s32[32,1,32]{2,1,0:T(1,128)} %bitcast.18), calls=%async_computation.1 | async-start | bytes 32768 | tf_op jit(solution)/shard_map/all_to_all | solution.py:160
  73.0 0.1 convolution_multiply_fusion.1
  73.1 0.1 fusion.77
  73.2 0.1 iota_compare_fusion.3
  73.3 0.0 copy-start.9
  73.4 0.0 copy-start.10
  73.4 0.7 fusion.80
  74.1 0.1 fusion.67
  74.2 0.2 fusion.42
  74.5 0.1 fusion.71
  74.6 0.2 fusion.69
  74.8 2.1 fusion.33
  76.8 0.6 copy.100
  77.5 1.0 multiply_cosine_fusion
  78.4 0.2 fusion.41
  78.7 1.4 all-to-all-done.1
  80.0 0.5 broadcast.446
  80.5 0.7 reduce.16
  81.2 0.1 reshape.594
  81.3 2.3 gather_fusion
  83.6 0.6 broadcast_select_fusion.2
  84.2 75.0 %all-gather.3.cloned.1.call-done = bf16[512,8192]{1,0:T(8,128)(2,1)} async-done(((bf16[512,1024]{1,0:T(8,128)(2,1)}), bf16[512,8192]{1,0:T(8,128)(2,1)}) %all-gather.3.cloned.1.call-update) | async-done | bytes 8388624 | tf_op jit(solution)/shard_map/all_gather | solution.py:183
  159.2 5.1 %fusion = f32[512]{0:T(512)S(1)} fusion(bf16[512,8192]{1,0:T(8,128)(2,1)} %all-gather.3.cloned.1.call-done), kind=kLoop, calls=%fused_computation.4 | loop fusion | flops 12582400 | bytes 8390656 | tf_op jit(solution)/shard_map/reduce_sum | solution.py:111
  164.3 83.7 %all-gather.5.cloned.1.call-done = bf16[8192,1280]{1,0:T(8,128)(2,1)} async-done(((bf16[256,1280]{1,0:T(8,128)(2,1)}), bf16[8192,1280]{1,0:T(8,128)(2,1)}) %all-gather.5.cloned.1.call-update) | async-done | bytes 20971536 | tf_op jit(solution)/shard_map/all_gather | solution.py:19
  248.0 15.0 %add_bitcast_fusion = f32[64,8,8,128]{3,1,2,0:T(8,128)S(1)} fusion(bf16[8192,1280]{1,0:T(8,128)(2,1)} %all-gather.5.cloned.1.call-done, bf16[512,8192]{1,0:T(8,128)(2,1)} %all-gather.3.cloned.1.call-done, f32[8192]{0:T(1024)S(1)} %copy-done.9, f32[512]{0:T(512)S(1)} %add_rsqrt_fusion, f32[1024]{0:T(1024)S(1)} %copy-done.10), kind=kOutput, calls=%fused_computation.30 | convolution fusion | flops 8607236096 | bytes 27301888 | tf_op jit(solution)/shard_map/dot_general | solution.py:191
  263.0 0.5 copy.118
  263.5 0.0 copy-start.6
  263.5 8.2 %fusion.10 = f32[512,256]{0,1:T(8,128)} fusion(bf16[8192,1280]{1,0:T(8,128)(2,1)} %all-gather.5.cloned.1.call-done, bf16[512,8192]{1,0:T(8,128)(2,1)} %all-gather.3.cloned.1.call-done, f32[8192]{0:T(1024)S(1)} %copy-done.9, f32[512]{0:T(512)S(1)} %add_rsqrt_fusion), kind=kOutput, calls=%fused_computation.18 | convolution fusion | flops 2164260864 | bytes 13142016 | tf_op jit(solution)/shard_map/dot_general | solution.py:191
  271.8 1.2 copy.95
  273.1 1.4 fusion.58
  274.5 0.7 fusion.79
  275.2 0.8 subtract_convert_fusion
  276.0 2.2 fusion.6
  278.2 1.7 fusion.5
  279.9 0.0 copy-start.1
  280.0 2.7 fusion.20
  282.6 1.3 copy.101
  (29 shorter events, 0.2 us)
Async XLA Ops:
  7.2 66.2 %copy-start = (bf16[2,4096,128]{2,1,0:T(8,128)(2,1)S(1)}, bf16[2,4096,128]{2,1,0:T(8,128)(2,1)}, u32[]{:S(2)}) copy-start(bf16[2,4096,128]{2,1,0:T(8,128)(2,1)} %param.17) | copy-start | bytes 6291460
  9.7 15.5 %all-to-all-start = ((s32[32,1,2]{2,1,0:T(1,128)}), s32[32,1,2]{2,1,0:T(1,128)S(1)}, u32[]{:S(2)}, u32[]{:S(2)}) async-start(s32[32,1,2]{2,1,0:T(1,128)} %copy.91), calls=%async_computation | async-start | bytes 32768 | tf_op jit(solution)/shard_map/all_to_all | solution.py:161
  22.9 42.1 %copy-start.2 = (bf16[256,2,128]{2,1,0:T(2,128)(2,1)S(1)}, bf16[256,2,128]{2,1,0:T(2,128)(2,1)}, u32[]{:S(2)}) copy-start(bf16[256,2,128]{2,1,0:T(2,128)(2,1)} %param.29) | copy-start | bytes 393220
  25.2 34.1 %all-to-all-start.2 = ((bf16[32,1,32,1024]{3,2,1,0:T(8,128)(2,1)}), bf16[32,1,32,1024]{3,2,1,0:T(8,128)(2,1)}, u32[]{:S(2)}, u32[]{:S(2)}) async-start(bf16[32,1,32,1024]{3,2,1,0:T(8,128)(2,1)} %copy.94), calls=%async_computation.2 | async-start | bytes 4194304 | tf_op jit(solution)/shard_map/all_to_all | solution.py:159
  30.5 36.5 %copy-start.5 = (s32[16]{0:T(128)S(1)}, s32[16]{0:T(128)}, u32[]{:S(2)}) copy-start(s32[16]{0:T(128)} %param.25) | copy-start | bytes 196
  30.5 36.6 %copy-start.3 = (s32[16,32]{1,0:T(8,128)S(1)}, s32[16,32]{1,0:T(8,128)}, u32[]{:S(2)}) copy-start(s32[16,32]{1,0:T(8,128)} %param.23) | copy-start | bytes 6148
  30.5 42.4 %copy-start.4 = (bf16[2,2,1024]{2,1,0:T(2,128)(2,1)S(1)}, bf16[2,2,1024]{2,1,0:T(2,128)(2,1)}, u32[]{:S(2)}) copy-start(bf16[2,2,1024]{2,1,0:T(2,128)(2,1)} %param.16) | copy-start | bytes 24580
  30.5 42.5 %copy-start.11 = (bf16[2,2,128]{2,1,0:T(2,128)(2,1)S(1)}, bf16[2,2,128]{2,1,0:T(2,128)(2,1)}, u32[]{:S(2)}) copy-start(bf16[2,2,128]{2,1,0:T(2,128)(2,1)} %param.19) | copy-start | bytes 3076
  30.5 42.7 %copy-start.8 = (s32[2]{0:T(128)S(1)}, s32[2]{0:T(128)}, u32[]{:S(2)}) copy-start(s32[2]{0:T(128)} %param.21) | copy-start | bytes 28
  30.6 128.6 %all-gather.3.cloned.1.call-start = ((), (), s32[]{:S(2)}) async-start(), calls=%async_computation.3 | async-start | bytes 9437184 | tf_op jit(solution)/shard_map/all_gather | solution.py:183
  59.2 15.3 %copy-start.7 = (bf16[2,2,128]{2,1,0:T(2,128)(2,1)S(1)}, bf16[2,2,128]{2,1,0:T(2,128)(2,1)}, u32[]{:S(2)}) copy-start(bf16[2,2,128]{2,1,0:T(2,128)(2,1)} %param.20) | copy-start | bytes 3076
  65.0 183.0 %all-gather.5.cloned.1.call-start = ((), (), s32[]{:S(2)}) async-start(), calls=%async_computation.4 | async-start | bytes 21626880 | tf_op jit(solution)/shard_map/all_gather | solution.py:19
  67.9 12.2 %all-to-all-start.1 = ((s32[32,1,32]{2,1,0:T(1,128)}), s32[32,1,32]{2,1,0:T(1,128)S(1)}, u32[]{:S(2)}, u32[]{:S(2)}) async-start(s32[32,1,32]{2,1,0:T(1,128)} %bitcast.18), calls=%async_computation.1 | async-start | bytes 32768 | tf_op jit(solution)/shard_map/all_to_all | solution.py:160
  73.3 174.7 %copy-start.9 = (f32[8192]{0:T(1024)S(1)}, f32[8192]{0:T(1024)}, u32[]{:S(2)}) copy-start(f32[8192]{0:T(1024)} %param.27) | copy-start | bytes 98308
  73.4 174.7 %copy-start.10 = (f32[1024]{0:T(1024)S(1)}, f32[1024]{0:T(1024)}, u32[]{:S(2)}) copy-start(f32[1024]{0:T(1024)} %param.30) | copy-start | bytes 12292
  263.5 9.5 %copy-start.6 = (f32[2,128]{1,0:T(2,128)S(1)}, f32[2,128]{1,0:T(2,128)}, u32[]{:S(2)}) copy-start(f32[2,128]{1,0:T(2,128)} %param.31) | copy-start | bytes 3076
  279.9 4.0 %copy-start.1 = (bf16[2,4096,128]{2,1,0:T(8,128)(2,1)S(1)}, bf16[2,4096,128]{2,1,0:T(8,128)(2,1)}, u32[]{:S(2)}) copy-start(bf16[2,4096,128]{2,1,0:T(8,128)(2,1)} %param.17) | copy-start | bytes 6291460
Sparse Core Ops, SparseCore 0:
  65.1 94.0 all-gather.2
  161.7 86.2 all-gather.4
where the time goes:
time: 291 us
  waiting for transfers between devices  189 us (65%)
  matrix products  33.4 us (11%)
  starting transfers between devices  19.1 us (7%)
  other arithmetic  18.1 us (6%)
  local copies, waits for them, and re-layouts  16.3 us (6%)
  between operations  14.4 us (5%)
    all_gather x1, waiting for transfers between devices, sent_together(): lax.all_gather(both, axis, axis=dim, tiled=True)  83.7 us
    all_gather x1, waiting for transfers between devices, on_device(): full_rows = lax.all_gather(tokens, 'tp', axis=1, tiled=True)  75 us
    all_to_all x1, waiting for transfers between devices, on_device(): lax.all_to_all(slot_rows, 'fsdp', split_axis=0, concat_axis=0, tiled=True)  27.1 us
    dot_general x2, matrix products, add_rows(): jnp.dot(columns, piece_rows, preferred_element_type=jnp.float32)  23.3 us
    all_to_all x1, starting transfers between devices, on_device(): lax.all_to_all(slot_meta, 'fsdp', split_axis=0, concat_axis=0, tiled=True)  8.58 us
  transfers between devices with their start and end apart: 5, of which 5 were waited for; matrix products, arithmetic and copies ran while one was open for 8% of the time, Pallas kernels for 0%

commit v1 on v0

--- a/solution.py
+++ b/solution.py
@@ -180,7 +180,9 @@
     tokens = jnp.where(covered[:, None], flat_rows[source_row], jnp.zeros((), jnp.bfloat16))
     packed_ids = jnp.where(covered, flat_ids[source_row], -1).astype(jnp.int32)
     doc_ids = jnp.where(covered, slot_pick, -1)
-    full_rows = lax.all_gather(tokens, "tp", axis=1, tiled=True)
+    full_rows = jnp.concatenate(
+        lax.all_to_all(jnp.stack([tokens] * lax.axis_size("tp")), "tp", 0, 0), axis=1
+    )
     scaled_input = normalize(full_rows, norm_gain)
     q_width = w_q.shape[1]
     pair_width = key_value_weight.shape[1] * key_value_weight.shape[2]

time: 291 us -> 355 us (1.22)
  local copies, waits for them, and re-layouts: 16.3 us -> 45.9 us
  waiting for transfers between devices: 189 us -> 210 us
  other arithmetic: 18.1 us -> 26.8 us
  starting transfers between devices: 19.1 us -> 25.7 us
    all_to_all x0 -> x1, waiting for transfers between devices: none -> 177 us  [on_device(): lax.all_to_all(jnp.stack([tokens] * lax.axis_size('tp')), 'tp', 0, 0)]
    all_gather x1, waiting for transfers between devices: 83.7 us -> 0.01 us  [sent_together(): lax.all_gather(both, axis, axis=dim, tiled=True)]
    all_gather x1 -> x0, waiting for transfers between devices: 75 us -> none  [on_device(): full_rows = lax.all_gather(tokens, 'tp', axis=1, tiled=True)]
    all_to_all x0 -> x1, local copies, waits for them, and re-layouts: none -> 11.4 us  [on_device(): lax.all_to_all(jnp.stack([tokens] * lax.axis_size('tp')), 'tp', 0, 0)]
    dot_general x0 -> x2, local copies, waits for them, and re-layouts: none -> 10.8 us  [add_rows(): jnp.dot(columns, piece_rows, preferred_element_type=jnp.float32)]
    all_to_all x0 -> x1, starting transfers between devices: none -> 7.39 us  [on_device(): lax.all_to_all(jnp.stack([tokens] * lax.axis_size('tp')), 'tp', 0, 0)]
    another operation x2 -> x3, other arithmetic: 0.9 us -> 5.34 us
    convert_element_type x0 -> x1, other arithmetic: none -> 4.44 us  [normalize(): return (wide * lax.rsqrt(jnp.mean(wide * wide, axis=1, keepdims=True) + e...]
  transfers between devices with their start and end apart: 5 -> 5, of which waited for: 5 -> 3; matrix products, arithmetic and copies ran while one was open for 8% -> 16% of each run, Pallas kernels for 0% -> 0%
where the time goes in v1:
time: 355 us; the launch traced here: 354 us
  waiting for transfers between devices  210 us (59%)
  local copies, waits for them, and re-layouts  45.9 us (13%)
  matrix products  31.7 us (9%)
  other arithmetic  26.8 us (8%)
  starting transfers between devices  25.7 us (7%)
  between operations  14.4 us (4%)
    all_to_all x1, waiting for transfers between devices, on_device(): lax.all_to_all(jnp.stack([tokens] * lax.axis_size('tp')), 'tp', 0, 0)  177 us
    all_to_all x1, waiting for transfers between devices, on_device(): lax.all_to_all(slot_rows, 'fsdp', split_axis=0, concat_axis=0, tiled=True)  30.4 us
    dot_general x2, matrix products, add_rows(): jnp.dot(columns, piece_rows, preferred_element_type=jnp.float32)  21.4 us
    all_to_all x1, local copies, waits for them, and re-layouts, on_device(): lax.all_to_all(jnp.stack([tokens] * lax.axis_size('tp')), 'tp', 0, 0)  11.4 us
    dot_general x2, local copies, waits for them, and re-layouts, add_rows(): jnp.dot(columns, piece_rows, preferred_element_type=jnp.float32)  10.8 us
    all_to_all x1, starting transfers between devices, on_device(): lax.all_to_all(slot_meta, 'fsdp', split_axis=0, concat_axis=0, tiled=True)  8.58 us
    all_to_all x1, starting transfers between devices, on_device(): lax.all_to_all(jnp.stack([tokens] * lax.axis_size('tp')), 'tp', 0, 0)  7.39 us
  transfers between devices with their start and end apart: 5, of which 3 were waited for; matrix products, arithmetic and copies ran while one was open for 16% of the time, Pallas kernels for 0%

profile of v1, /device:TPU:1, one launch (start us, length us, event | category | flops | bytes accessed | tf_op | source)
XLA Modules:
  0.0 354.3 jit_solution(3487129687991338225)
XLA Ops:
  7.2 0.0 copy-start
  7.2 0.0 copy-start.8
  7.2 0.0 all-gather.2.cloned.1.call-start
  7.2 1.1 copy.151
  8.3 1.9 pad_maximum_fusion
  10.3 0.0 all-gather.2.cloned.1.call-update
  10.3 0.9 convert_reduce_fusion
  11.2 0.8 select_reduce_fusion.4
  12.0 0.7 copy.93
  12.7 8.6 %all-to-all-start = ((s32[32,1,2]{2,1,0:T(1,128)}), s32[32,1,2]{2,1,0:T(1,128)S(1)}, u32[]{:S(2)}, u32[]{:S(2)}) async-start(s32[32,1,2]{2,1,0:T(1,128)} %copy.93), calls=%async_computation | async-start | bytes 32768 | tf_op jit(solution)/shard_map/all_to_all | solution.py:161
  21.3 2.2 convert_bitcast_fusion
  23.5 2.5 copy.96
  26.0 2.2 all-to-all-done
  28.2 5.2 %all-to-all-start.2 = ((bf16[32,1,32,1024]{3,2,1,0:T(8,128)(2,1)}), bf16[32,1,32,1024]{3,2,1,0:T(8,128)(2,1)}, u32[]{:S(2)}, u32[]{:S(2)}) async-start(bf16[32,1,32,1024]{3,2,1,0:T(8,128)(2,1)} %copy.96), calls=%async_computation.2 | async-start | bytes 4194304 | tf_op jit(solution)/shard_map/all_to_all | solution.py:159
  33.4 0.1 fusion.56
  33.5 0.7 select_reduce_fusion
  34.2 1.3 slice_reduce_fusion
  35.5 0.1 fusion.53
  35.6 0.1 select_reduce_fusion.1
  35.8 30.4 %all-to-all-done.2 = bf16[32,1,32,1024]{3,2,1,0:T(8,128)(2,1)} async-done(((bf16[32,1,32,1024]{3,2,1,0:T(8,128)(2,1)}), bf16[32,1,32,1024]{3,2,1,0:T(8,128)(2,1)}, u32[]{:S(2)}, u32[]{:S(2)}) %all-to-all-start.2) | async-done | bytes 2097184 | tf_op jit(solution)/shard_map/all_to_all | solution.py:159
  66.2 4.4 %all-to-all-start.1 = ((s32[32,1,32]{2,1,0:T(1,128)}), s32[32,1,32]{2,1,0:T(1,128)S(1)}, u32[]{:S(2)}, u32[]{:S(2)}) async-start(s32[32,1,32]{2,1,0:T(1,128)} %bitcast.18), calls=%async_computation.1 | async-start | bytes 32768 | tf_op jit(solution)/shard_map/all_to_all | solution.py:160
  70.7 5.3 %gather_fusion.1 = bf16[512,1024]{1,0:T(8,128)(2,1)} fusion(bf16[1024,1024]{1,0:T(8,128)(2,1)} %bitcast.24, s32[1024]{0:T(1024)S(1)} %pad_clamp_fusion), kind=kCustom, calls=%fused_computation.1 | custom fusion | bytes 2099200 | tf_op jit(solution)/shard_map/gather | solution.py:180
  76.0 1.7 broadcast_select_fusion
  77.7 0.0 all-to-all-done.1
  77.7 4.4 %stack.11 = bf16[8,512,1024]{2,1,0:T(8,128)(2,1)} broadcast(bf16[512,1024]{1,0:T(8,128)(2,1)S(1)} %broadcast_select_fusion), dimensions={1,2} | broadcast | bytes 9437184 | tf_op jit(solution)/shard_map/stack | solution.py:184
  82.1 0.0 copy-start.5
  82.1 7.4 %all-to-all-start.3 = ((bf16[8,512,1024]{2,1,0:T(8,128)(2,1)}), bf16[8,512,1024]{2,1,0:T(8,128)(2,1)}, u32[]{:S(2)}, u32[]{:S(2)}) async-start(bf16[8,512,1024]{2,1,0:T(8,128)(2,1)} %stack.11), calls=%async_computation.3 | async-start | bytes 16777216 | tf_op jit(solution)/shard_map/all_to_all | solution.py:184
  89.5 0.0 copy-done.7
  89.6 0.1 convolution_multiply_fusion.1
  89.7 0.1 fusion.70
  89.8 0.1 iota_compare_fusion.3
  89.9 0.7 fusion.73
  90.7 0.1 fusion.60
  90.8 0.2 fusion.35
  91.0 0.1 fusion.64
  91.1 0.2 fusion.62
  91.3 2.1 fusion.26
  93.4 0.6 copy.104
  94.0 0.2 fusion.34
  94.2 1.0 multiply_cosine_fusion
  95.2 0.5 broadcast.458
  95.7 0.7 reduce.18
  96.4 0.1 reshape.616
  96.5 2.3 gather_fusion
  98.8 0.6 broadcast_select_fusion.2
  99.4 177.2 %all-to-all-done.3 = bf16[8,512,1024]{2,1,0:T(8,128)(2,1)} async-done(((bf16[8,512,1024]{2,1,0:T(8,128)(2,1)}), bf16[8,512,1024]{2,1,0:T(8,128)(2,1)}, u32[]{:S(2)}, u32[]{:S(2)}) %all-to-all-start.3) | async-done | bytes 8388640 | tf_op jit(solution)/shard_map/all_to_all | solution.py:184
  276.6 11.4 %copy.97 = bf16[8,512,1024]{1,2,0:T(8,128)(2,1)} copy(bf16[8,512,1024]{2,1,0:T(8,128)(2,1)} %all-to-all-done.3) | data formatting | bytes 16777216 | tf_op jit(solution)/shard_map/all_to_all | solution.py:184
  288.0 5.3 %multiply_reduce_fusion = f32[512]{0:T(512)S(1)} fusion(bf16[8,512,1024]{1,2,0:T(8,128)(2,1)} %copy.97), kind=kLoop, calls=%fused_computation.8 | loop fusion | flops 12582400 | bytes 8390656 | tf_op jit(solution)/shard_map/reduce_sum | solution.py:111
  293.3 0.4 copy-done.2
  293.7 4.4 %multiply_convert_fusion = bf16[8,512,1024]{1,2,0:T(8,128)(2,1)} fusion(f32[8,1024]{1,0:T(8,128)S(1)} %mul.182, f32[512]{0:T(512)S(1)} %add_rsqrt_fusion, bf16[8,512,1024]{1,2,0:T(8,128)(2,1)S(1)} %copy-done.2), kind=kLoop, calls=%fused_computation.7 | loop fusion | flops 16777216 | bytes 16812032 | tf_op jit(solution)/shard_map/convert.9
  298.2 4.4 %fusion.3 = bf16[512,8192]{0,1:T(8,128)(2,1)} fusion(f32[8192]{0:T(1024)S(1)} %copy-done.5, f32[512]{0:T(512)S(1)} %add_rsqrt_fusion, bf16[8,512,1024]{1,2,0:T(8,128)(2,1)S(1)} %copy-done.2), kind=kLoop, calls=%fused_computation.6 | loop fusion | flops 16777216 | bytes 16812032 | tf_op jit(solution)/shard_map/convert_element_type | solution.py:113
  302.6 14.4 %add_bitcast_fusion = f32[64,8,8,128]{3,1,2,0:T(8,128)S(1)} fusion(bf16[512,8192]{0,1:T(8,128)(2,1)} %fusion.3, bf16[8192,1280]{1,0:T(8,128)(2,1)} %all-gather.2.cloned.1.call-done, f32[1024]{0:T(1024)S(1)} %copy-done.11), kind=kOutput, calls=%fused_computation.29 | convolution fusion | flops 8590458880 | bytes 27267072 | tf_op jit(solution)/shard_map/dot_general | solution.py:193
  317.0 0.5 copy.124
  317.5 2.7 fusion.72
  320.2 4.4 %slice_bitcast_fusion = bf16[256,8192]{0,1:T(8,128)(2,1)} fusion(bf16[8192,1280]{1,0:T(8,128)(2,1)} %all-gather.2.cloned.1.call-done), kind=kLoop, calls=%fused_computation.18 | loop fusion | bytes 8388608 | tf_op jit(solution)/shard_map/dot_general | solution.py:193
  324.6 6.4 %copy.98 = bf16[256,8192]{1,0:T(8,128)(2,1)} copy(bf16[256,8192]{0,1:T(8,128)(2,1)} %slice_bitcast_fusion) | data formatting | bytes 8388608 | tf_op jit(solution)/shard_map/dot_general | solution.py:193
  331.0 7.0 %convolution_add_fusion = f32[512,2,128]{0,2,1:T(8,128)S(1)} fusion(bf16[512,8192,1]{0,1,2:T(8,128)(2,1)} %bitcast.134, bf16[2,128,8192]{2,1,0:T(8,128)(2,1)} %bitcast.135, f32[2,128]{1,0:T(2,128)S(1)} %copy-done.13), kind=kOutput, calls=%fused_computation.31 | convolution fusion | flops 2147614720 | bytes 13108224 | tf_op jit(solution)/shard_map/dot_general | solution.py:193
  338.0 0.6 fusion.51
  338.6 0.8 subtract_convert_fusion
  339.4 2.2 fusion.5
  341.7 1.7 fusion.4
  343.4 0.0 copy-start.1
  343.4 2.7 fusion.15
  346.2 1.3 copy.105
  (37 shorter events, 0.2 us)
Async XLA Ops:
  7.2 82.7 %copy-start = (bf16[2,4096,128]{2,1,0:T(8,128)(2,1)S(1)}, bf16[2,4096,128]{2,1,0:T(8,128)(2,1)}, u32[]{:S(2)}) copy-start(bf16[2,4096,128]{2,1,0:T(8,128)(2,1)} %param.17) | copy-start | bytes 6291460
  7.2 26.2 %copy-start.8 = (s32[16]{0:T(128)S(1)}, s32[16]{0:T(128)}, u32[]{:S(2)}) copy-start(s32[16]{0:T(128)} %param.25) | copy-start | bytes 196
  7.2 26.3 %copy-start.6 = (s32[16,32]{1,0:T(8,128)S(1)}, s32[16,32]{1,0:T(8,128)}, u32[]{:S(2)}) copy-start(s32[16,32]{1,0:T(8,128)} %param.23) | copy-start | bytes 6148
  7.2 295.4 %all-gather.2.cloned.1.call-start = ((), (), s32[]{:S(2)}) async-start(), calls=%async_computation.4 | async-start | bytes 21626880 | tf_op jit(solution)/shard_map/all_gather | solution.py:19
  12.7 15.5 %all-to-all-start = ((s32[32,1,2]{2,1,0:T(1,128)}), s32[32,1,2]{2,1,0:T(1,128)S(1)}, u32[]{:S(2)}, u32[]{:S(2)}) async-start(s32[32,1,2]{2,1,0:T(1,128)} %copy.93), calls=%async_computation | async-start | bytes 32768 | tf_op jit(solution)/shard_map/all_to_all | solution.py:161
  28.2 38.0 %all-to-all-start.2 = ((bf16[32,1,32,1024]{3,2,1,0:T(8,128)(2,1)}), bf16[32,1,32,1024]{3,2,1,0:T(8,128)(2,1)}, u32[]{:S(2)}, u32[]{:S(2)}) async-start(bf16[32,1,32,1024]{3,2,1,0:T(8,128)(2,1)} %copy.96), calls=%async_computation.2 | async-start | bytes 4194304 | tf_op jit(solution)/shard_map/all_to_all | solution.py:159
  66.2 11.5 %all-to-all-start.1 = ((s32[32,1,32]{2,1,0:T(1,128)}), s32[32,1,32]{2,1,0:T(1,128)S(1)}, u32[]{:S(2)}, u32[]{:S(2)}) async-start(s32[32,1,32]{2,1,0:T(1,128)} %bitcast.18), calls=%async_computation.1 | async-start | bytes 32768 | tf_op jit(solution)/shard_map/all_to_all | solution.py:160
  82.1 7.4 %copy-start.7 = (bf16[2,2,1024]{2,1,0:T(2,128)(2,1)S(1)}, bf16[2,2,1024]{2,1,0:T(2,128)(2,1)}, u32[]{:S(2)}) copy-start(bf16[2,2,1024]{2,1,0:T(2,128)(2,1)} %param.16) | copy-start | bytes 24580
  82.1 7.5 %copy-start.12 = (bf16[2,2,128]{2,1,0:T(2,128)(2,1)S(1)}, bf16[2,2,128]{2,1,0:T(2,128)(2,1)}, u32[]{:S(2)}) copy-start(bf16[2,2,128]{2,1,0:T(2,128)(2,1)} %param.19) | copy-start | bytes 3076
  82.1 7.7 %copy-start.10 = (s32[2]{0:T(128)S(1)}, s32[2]{0:T(128)}, u32[]{:S(2)}) copy-start(s32[2]{0:T(128)} %param.21) | copy-start | bytes 28
  82.1 9.0 %copy-start.9 = (bf16[2,2,128]{2,1,0:T(2,128)(2,1)S(1)}, bf16[2,2,128]{2,1,0:T(2,128)(2,1)}, u32[]{:S(2)}) copy-start(bf16[2,2,128]{2,1,0:T(2,128)(2,1)} %param.20) | copy-start | bytes 3076
  82.1 11.9 %copy-start.5 = (f32[8192]{0:T(1024)S(1)}, f32[8192]{0:T(1024)}, u32[]{:S(2)}) copy-start(f32[8192]{0:T(1024)} %param.27) | copy-start | bytes 98308
  82.1 194.5 %all-to-all-start.3 = ((bf16[8,512,1024]{2,1,0:T(8,128)(2,1)}), bf16[8,512,1024]{2,1,0:T(8,128)(2,1)}, u32[]{:S(2)}, u32[]{:S(2)}) async-start(bf16[8,512,1024]{2,1,0:T(8,128)(2,1)} %stack.11), calls=%async_computation.3 | async-start | bytes 16777216 | tf_op jit(solution)/shard_map/all_to_all | solution.py:184
  288.0 5.8 %copy-start.2 = (bf16[8,512,1024]{1,2,0:T(8,128)(2,1)S(1)}, bf16[8,512,1024]{1,2,0:T(8,128)(2,1)}, u32[]{:S(2)}) copy-start(bf16[8,512,1024]{1,2,0:T(8,128)(2,1)} %copy.97) | copy-start | bytes 25165828
  298.2 4.4 %copy-start.11 = (f32[1024]{0:T(1024)S(1)}, f32[1024]{0:T(1024)}, u32[]{:S(2)}) copy-start(f32[1024]{0:T(1024)} %param.30) | copy-start | bytes 12292
  320.2 10.8 %copy-start.13 = (f32[2,128]{1,0:T(2,128)S(1)}, f32[2,128]{1,0:T(2,128)}, u32[]{:S(2)}) copy-start(f32[2,128]{1,0:T(2,128)} %param.31) | copy-start | bytes 3076
  331.0 7.6 %copy-start.3 = (f32[512,8,64]{2,1,0:T(8,128)S(1)}, f32[512,8,64]{2,1,0:T(8,128)}, u32[]{:S(2)}) copy-start(f32[512,8,64]{2,1,0:T(8,128)} %get-tuple-element.26) | copy-start | bytes 3145732
  331.0 7.6 %copy-start.4 = (f32[512,8,64]{2,1,0:T(8,128)S(1)}, f32[512,8,64]{2,1,0:T(8,128)}, u32[]{:S(2)}) copy-start(f32[512,8,64]{2,1,0:T(8,128)} %get-tuple-element.27) | copy-start | bytes 3145732
  343.4 4.1 %copy-start.1 = (bf16[2,4096,128]{2,1,0:T(8,128)(2,1)S(1)}, bf16[2,4096,128]{2,1,0:T(8,128)(2,1)}, u32[]{:S(2)}) copy-start(bf16[2,4096,128]{2,1,0:T(8,128)(2,1)} %param.17) | copy-start | bytes 6291460
Sparse Core Ops, SparseCore 0:
  10.6 112.9 all-gather.1
